TPU v7x, 128 devices: a whole 4x4x4 slice. The times are simulated.
128 devices in a mesh: sample: 8 (over z_lo, y), feat: 16 (over x, z_hi, core).
Axes of the slice: x: 4, y: 4, z: 4 (z_hi: 2, z_lo: 2; z = z_hi * 2 + z_lo), core: 2. Of those that a mesh axis runs over, the one named last changes fastest.
Arguments:
- view_a: bfloat16 [1024, 16384], P('sample', 'feat'), may hold values from -60 to 60
- view_b: bfloat16 [1024, 16384], P('sample', 'feat'), may hold values from -60 to 60
Outputs:
- loss: float32 [], replicated
- grad_a: bfloat16 [1024, 16384], P('sample', 'feat')
- grad_b: bfloat16 [1024, 16384], P('sample', 'feat')
All inputs are finite; a program needn't handle non-finite values.
Results may differ from a plain program's by a relative error of at most 0.02.
Values may be sent and summed in bfloat16 or wider, within the bound.
No kernel may reach another device: no remote copies, remote signals or barrier semaphores. Data moves between devices by JAX's collectives and lax.ppermute only.
A program may use at most 64 MiB of HBM per device.

v0:
```python
import jax
import jax.numpy as jnp
from jax import lax
from jax.sharding import PartitionSpec as P

EPSILON = 1e-05
OFF_WEIGHT = 0.0051


def body(view_a, view_b):
    rows_dev, cols_dev = view_a.shape
    groups = lax.axis_size("sample")
    blocks = lax.axis_size("feat")
    total_rows = rows_dev * groups
    sub_width = cols_dev // groups
    inv_rows = 1.0 / total_rows
    sample_id = lax.axis_index("sample")
    feat_id = lax.axis_index("feat")
    float_a = view_a.astype(jnp.float32)
    float_b = view_b.astype(jnp.float32)
    moment_sums = lax.psum(
        (
            jnp.sum(float_a, axis=0),
            jnp.sum(float_a * float_a, axis=0),
            jnp.sum(float_b, axis=0),
            jnp.sum(float_b * float_b, axis=0),
        ),
        "sample",
    )
    mean_a = moment_sums[0] * inv_rows
    scale_a = lax.rsqrt(moment_sums[1] * inv_rows - mean_a * mean_a + EPSILON)
    mean_b = moment_sums[2] * inv_rows
    scale_block_b = lax.rsqrt(moment_sums[3] * inv_rows - mean_b * mean_b + EPSILON)
    local_a = ((float_a - mean_a) * scale_a).astype(jnp.bfloat16)
    source_b = ((float_b - mean_b) * scale_block_b).astype(jnp.bfloat16)
    scale_b = lax.dynamic_slice_in_dim(scale_block_b, sample_id * sub_width, sub_width)
    norm_a = lax.all_gather(local_a, "sample", axis=0, tiled=True)
    row_index = jnp.arange(cols_dev, dtype=jnp.int32)
    wide_b = lax.all_gather(source_b, "feat", axis=1, tiled=True)
    arranged = (
        wide_b.reshape(rows_dev, blocks, groups, sub_width)
        .transpose(0, 2, 1, 3)
        .reshape(rows_dev, blocks * cols_dev)
    )
    moved_b = lax.all_to_all(arranged, "sample", split_axis=1, concat_axis=0, tiled=True)
    own_b = lax.dynamic_slice_in_dim(moved_b, feat_id * sub_width, sub_width, 1)
    panel_width = moved_b.shape[1]
    correlation = (
        lax.dot_general(
            norm_a, moved_b, (((0,), (0,)), ((), ())), preferred_element_type=jnp.float32
        )
        * inv_rows
    )
    local_cols = jnp.arange(panel_width, dtype=jnp.int32)
    owner_block = local_cols // sub_width
    offset = local_cols % sub_width
    on_diagonal = (owner_block[None, :] == feat_id) & (
        offset[None, :] + sample_id * sub_width == row_index[:, None]
    )
    missing = 1.0 - correlation
    piece_loss = jnp.sum(
        jnp.where(on_diagonal, missing * missing, OFF_WEIGHT * correlation * correlation)
    )
    factor = jnp.where(on_diagonal, correlation - 1.0, OFF_WEIGHT * correlation).astype(
        jnp.bfloat16
    )
    grad_rows = lax.dot_general(
        moved_b, factor, (((1,), (1,)), ((), ())), preferred_element_type=jnp.float32
    )
    folded = (piece_loss, grad_rows, factor)
    loss_sum, grad_rows, factor_tile = folded
    row_grad = lax.psum_scatter(
        grad_rows.astype(jnp.bfloat16), "sample", scatter_dimension=0, tiled=True
    ).astype(jnp.float32)
    float_local = local_a.astype(jnp.float32)
    moments = lax.psum(
        (jnp.sum(row_grad, axis=0), jnp.sum(row_grad * float_local, axis=0)), "sample"
    )
    grad_a = (
        scale_a * (row_grad - moments[0] * inv_rows - float_local * (moments[1] * inv_rows))
    ).astype(jnp.bfloat16)
    col_grad = lax.psum_scatter(
        lax.dot_general(
            factor_tile, norm_a, (((0,), (1,)), ((), ())), preferred_element_type=jnp.float32
        ).astype(jnp.bfloat16),
        "feat",
        scatter_dimension=0,
        tiled=True,
    ).astype(jnp.float32)
    own_t = own_b.T.astype(jnp.float32)
    mean_grad = jnp.mean(col_grad, axis=1, keepdims=True)
    mean_cross = jnp.mean(col_grad * own_t, axis=1, keepdims=True)
    grad_b_t = (scale_b[:, None] * (col_grad - mean_grad - own_t * mean_cross)).astype(jnp.bfloat16)
    returned = lax.all_to_all(grad_b_t, "sample", split_axis=1, concat_axis=0, tiled=True)
    grad_b = returned.T
    loss = lax.psum(loss_sum, ("sample", "feat")) / (cols_dev * blocks)
    return (loss, grad_a, grad_b)


def solution(mesh):
    in_specs = (P("sample", "feat"), P("sample", "feat"))
    out_specs = (P(), P("sample", "feat"), P("sample", "feat"))
    return jax.shard_map(body, mesh=mesh, in_specs=in_specs, out_specs=out_specs, check_vma=False)
```

profile of v0, /device:TPU:0, one launch (start us, length us, event | category | flops | bytes accessed | tf_op | source)
XLA Modules:
  0.0 370.2 jit_solution(4005084618769182151)
XLA Ops:
  7.2 1.2 convert_reduce_fusion.2
  8.4 34.9 %all-reduce.1 = (f32[1024]{0:T(1024)S(1)}, f32[1024]{0:T(1024)S(1)}, f32[1024]{0:T(1024)S(1)}, f32[1024]{0:T(1024)S(1)}) all-reduce(f32[1024]{0:T(1024)S(1)} %get-tuple-element.23, f32[1024]{0:T(1024)S(1)} %get-tuple-element.24, f32[1024]{0:T(1024)S(1)} %get-tuple-element.8, ...), channel_id=1, replica_groups=mesh['sample'=8,'feat'=16] {'sample'}, use_global_device_ids=true, to_apply=%region_3.0 | all-reduce | flops 4096 | bytes 32768 | tf_op jit(solution)/shard_map/psum | solution.py:21
  43.4 1.7 fusion.8
  45.2 1.7 fusion.5
  46.9 53.7 %all-gather.5.cloned.1.call-done = bf16[128,16384]{1,0:T(8,128)(2,1)} async-done(((bf16[128,1024]{1,0:T(8,128)(2,1)}), bf16[128,16384]{1,0:T(8,128)(2,1)}) %all-gather.5.cloned.1.call-update) | async-done | bytes 4194320 | tf_op jit(solution)/shard_map/all_gather | solution.py:39
  100.6 5.4 %copy.13 = bf16[16,8,128,128]{3,2,1,0:T(8,128)(2,1)} copy(bf16[16,8,128,128]{3,1,2,0:T(8,128)(2,1)} %bitcast.43) | data formatting | bytes 8388608
  106.0 6.9 %copy.7 = bf16[128,16,8,128]{0,3,1,2:T(8,128)(2,1)} copy(bf16[128,16,8,128]{3,2,1,0:T(8,128)(2,1)} %bitcast.42) | data formatting | bytes 8388608 | tf_op jit(solution)/shard_map/reshape | solution.py:41
  112.9 4.6 %all-to-all-start = ((bf16[128,8,2048]{0,2,1:T(8,128)(2,1)}), bf16[128,8,2048]{0,2,1:T(8,128)(2,1)}, u32[]{:S(2)}, u32[]{:S(2)}) async-start(bf16[128,8,2048]{0,2,1:T(8,128)(2,1)} %bitcast.41), calls=%async_computation | async-start | bytes 8388608 | tf_op jit(solution)/shard_map/all_to_all | solution.py:45
  117.6 80.9 %all-gather.3.cloned.1.call-done = bf16[1024,1024]{1,0:T(8,128)(2,1)} async-done(((bf16[128,1024]{1,0:T(8,128)(2,1)}), bf16[1024,1024]{1,0:T(8,128)(2,1)}) %all-gather.3.cloned.1.call-update) | async-done | bytes 2097168 | tf_op jit(solution)/shard_map/all_gather | solution.py:37
  198.5 9.5 %select_reduce_fusion = (f32[]{:T(128)}, f32[1024,2048]{1,0:T(8,128)S(1)}) fusion(s32[2048]{0:T(1024)S(1)} %fusion.23, pred[2048]{0:T(1024)(128)(4,1)S(1)} %fusion.22, bf16[1024,1024]{1,0:T(8,128)(2,1)} %all-gather.3.cloned.1.call-done, bf16[128,8,2048]{0,2,1:T(8,128)(2,1)} %all-to-all-done), kind=kOutput, calls=%fused_computation.1 | convolution fusion | flops 4313841664 | bytes 14690308 | tf_op jit(solution)/shard_map/dot_general | solution.py:49
  208.0 3.2 copy-done.2
  211.2 8.4 %convolution_convert_fusion.1 = bf16[1024,1024]{1,0:T(8,128)(2,1)} fusion(f32[1024,2048]{1,0:T(8,128)S(1)} %get-tuple-element.22, s32[2048]{0:T(1024)S(1)} %fusion.23, pred[2048]{0:T(1024)(128)(4,1)S(1)} %fusion.22, bf16[128,8,2048]{0,2,1:T(8,128)(2,1)} %all-to-all-done), kind=kOutput, calls=%fused_computation.6 | convolution fusion | flops 4310695936 | bytes 14690304 | tf_op jit(solution)/shard_map/dot_general | solution.py:67
  219.7 12.0 %convolution_convert_fusion = bf16[2048,1024]{1,0:T(8,128)(2,1)} fusion(bf16[1024,1024]{1,0:T(8,128)(2,1)S(1)} %copy-done.1, f32[1024,2048]{1,0:T(8,128)} %copy-done.2, s32[2048]{0:T(1024)S(1)} %fusion.23, pred[2048]{0:T(1024)(128)(4,1)S(1)} %fusion.22), kind=kOutput, calls=%fused_computation.5 | convolution fusion | flops 4311744512 | bytes 14690304 | tf_op jit(solution)/shard_map/dot_general | solution.py:83
  231.8 65.5 %psum.53 = f32[]{:T(128)} all-reduce(f32[]{:T(128)} %get-tuple-element.21), channel_id=1, replica_groups=mesh['sample'=8,'feat'=16] {'sample','feat'}, use_global_device_ids=true, to_apply=%region_9.10 | all-reduce | flops 1 | bytes 8 | tf_op jit(solution)/shard_map/psum | solution.py:96
  298.0 4.8 %copy_bitcast_fusion = bf16[1024,2048]{0,1:T(8,128)(2,1)} fusion(bf16[128,8,2048]{0,2,1:T(8,128)(2,1)} %all-to-all-done), kind=kLoop, calls=%fused_computation.4 | loop fusion | bytes 8388608 | tf_op jit(solution)/shard_map/all_to_all | solution.py:45
  302.8 1.1 convert_reduce_fusion.1
  303.9 17.7 %all-reduce = (f32[1024]{0:T(1024)S(1)}, f32[1024]{0:T(1024)S(1)}) all-reduce(f32[1024]{0:T(1024)S(1)} %get-tuple-element.6, f32[1024]{0:T(1024)S(1)} %get-tuple-element.5), channel_id=1, replica_groups=mesh['sample'=8,'feat'=16] {'sample'}, use_global_device_ids=true, to_apply=%region_14.15 | all-reduce | flops 2048 | bytes 16384 | tf_op jit(solution)/shard_map/psum | solution.py:76
  321.7 25.1 %reduce-scatter.5.cloned.1.call-done = bf16[128,1024]{1,0:T(8,128)(2,1)} async-done(((bf16[2048,1024]{1,0:T(8,128)(2,1)}), bf16[128,1024]{1,0:T(8,128)(2,1)}) %reduce-scatter.5.cloned.1.call-update) | async-done | bytes 262160 | tf_op jit(solution)/shard_map/reduce_scatter | solution.py:82
  346.8 1.2 convert_reduce_fusion
  348.0 2.0 copy_bitcast_fusion.1
  350.0 4.4 %all-to-all-start.1 = ((bf16[128,8,128]{2,0,1:T(8,128)(2,1)}), bf16[128,8,128]{2,0,1:T(8,128)(2,1)S(1)}, u32[]{:S(2)}, u32[]{:S(2)}) async-start(bf16[128,8,128]{2,0,1:T(8,128)(2,1)} %copy_bitcast_fusion.1), calls=%async_computation.3 | async-start | bytes 524288 | tf_op jit(solution)/shard_map/all_to_all | solution.py:94
  354.4 1.8 fusion.3
  356.2 5.5 %all-to-all-done.1 = bf16[128,8,128]{2,0,1:T(8,128)(2,1)S(1)} async-done(((bf16[128,8,128]{2,0,1:T(8,128)(2,1)}), bf16[128,8,128]{2,0,1:T(8,128)(2,1)S(1)}, u32[]{:S(2)}, u32[]{:S(2)}) %all-to-all-start.1) | async-done | bytes 262176 | tf_op jit(solution)/shard_map/all_to_all | solution.py:94
  361.7 0.8 copy.10
  (24 shorter events, 0.4 us)
Async XLA Ops:
  7.2 93.5 %all-gather.5.cloned.1.call-start = ((), (), s32[]{:S(2)}) async-start(), calls=%async_computation.5 | async-start | bytes 4456448 | tf_op jit(solution)/shard_map/all_gather | solution.py:39
  45.1 153.4 %all-gather.3.cloned.1.call-start = ((), (), s32[]{:S(2)}) async-start(), calls=%async_computation.4 | async-start | bytes 2359296 | tf_op jit(solution)/shard_map/all_gather | solution.py:37
  112.9 85.6 %all-to-all-start = ((bf16[128,8,2048]{0,2,1:T(8,128)(2,1)}), bf16[128,8,2048]{0,2,1:T(8,128)(2,1)}, u32[]{:S(2)}, u32[]{:S(2)}) async-start(bf16[128,8,2048]{0,2,1:T(8,128)(2,1)} %bitcast.41), calls=%async_computation | async-start | bytes 8388608 | tf_op jit(solution)/shard_map/all_to_all | solution.py:45
  117.5 185.3 %reduce-scatter.3.cloned.1.call-start = ((), (), s32[]{:S(2)}) async-start(), calls=%async_computation.6 | async-start | bytes 2359296 | tf_op jit(solution)/shard_map/reduce_scatter | solution.py:72
  208.0 3.2 copy-start.2
  211.2 8.5 %copy-start.1 = (bf16[1024,1024]{1,0:T(8,128)(2,1)S(1)}, bf16[1024,1024]{1,0:T(8,128)(2,1)}, u32[]{:S(2)}) copy-start(bf16[1024,1024]{1,0:T(8,128)(2,1)} %all-gather.3.cloned.1.call-done) | copy-start | bytes 6291460
  219.7 127.1 %reduce-scatter.5.cloned.1.call-start = ((), (), s32[]{:S(2)}) async-start(), calls=%async_computation.7 | async-start | bytes 4456448 | tf_op jit(solution)/shard_map/reduce_scatter | solution.py:82
  298.0 4.8 %copy-start = (bf16[128,1024]{1,0:T(8,128)(2,1)S(1)}, bf16[128,1024]{1,0:T(8,128)(2,1)}, u32[]{:S(2)}) copy-start(bf16[128,1024]{1,0:T(8,128)(2,1)} %param.2) | copy-start | bytes 786436
  350.0 11.7 %all-to-all-start.1 = ((bf16[128,8,128]{2,0,1:T(8,128)(2,1)}), bf16[128,8,128]{2,0,1:T(8,128)(2,1)S(1)}, u32[]{:S(2)}, u32[]{:S(2)}) async-start(bf16[128,8,128]{2,0,1:T(8,128)(2,1)} %copy_bitcast_fusion.1), calls=%async_computation.3 | async-start | bytes 524288 | tf_op jit(solution)/shard_map/all_to_all | solution.py:94
Sparse Core Ops, SparseCore 0:
  45.2 55.3 all-gather.4
  102.8 95.5 all-gather.2
  219.8 43.6 reduce-scatter.2
  267.4 79.3 reduce-scatter.4
where the time goes:
time: 371 us; the launch traced here: 370 us
  waiting for transfers between devices  165 us (44%)
  blocking collectives  118 us (32%)
  matrix products  29.9 us (8%)
  local copies, waits for them, and re-layouts  21.2 us (6%)
  between operations  15.6 us (4%)
  other arithmetic  10.8 us (3%)
  starting transfers between devices  9.14 us (2%)
    all_gather x1, waiting for transfers between devices, body(): norm_a = lax.all_gather(local_a, 'sample', axis=0, tiled=True)  80.9 us
    psum x1, blocking collectives, body(): loss = lax.psum(loss_sum, ('sample', 'feat')) / (cols_dev * blocks)  65.5 us
    all_gather x1, waiting for transfers between devices, body(): wide_b = lax.all_gather(source_b, 'feat', axis=1, tiled=True)  53.7 us
    psum x1, blocking collectives, body(): lax.psum((jnp.sum(float_a, axis=0), jnp.sum(float_a * float_a, axis=0), j...  34.9 us
    reduce_scatter x1, waiting for transfers between devices, body(): lax.psum_scatter(lax.dot_general(factor_tile, norm_a, (((0,), (1,)), ((),...  25.1 us
    psum x1, blocking collectives, body(): lax.psum((jnp.sum(row_grad, axis=0), jnp.sum(row_grad * float_local, axis...  17.7 us
    dot_general x1, matrix products, body(): lax.dot_general(factor_tile, norm_a, (((0,), (1,)), ((), ())), preferred_...  12 us
    dot_general x1, matrix products, body(): lax.dot_general(norm_a, moved_b, (((0,), (0,)), ((), ())), preferred_elem...  9.54 us
  transfers between devices with their start and end apart: 6, of which 4 were waited for; matrix products, arithmetic and copies ran while one was open for 9% of the time, Pallas kernels for 0%

commit v1 on v0

--- a/solution.py
+++ b/solution.py
@@ -91,7 +91,12 @@
     mean_grad = jnp.mean(col_grad, axis=1, keepdims=True)
     mean_cross = jnp.mean(col_grad * own_t, axis=1, keepdims=True)
     grad_b_t = (scale_b[:, None] * (col_grad - mean_grad - own_t * mean_cross)).astype(jnp.bfloat16)
-    returned = lax.all_to_all(grad_b_t, "sample", split_axis=1, concat_axis=0, tiled=True)
+    returned = jnp.concatenate(
+        lax.all_to_all(
+            jnp.stack(jnp.split(grad_b_t, lax.axis_size("sample"), axis=1)), "sample", 0, 0
+        ),
+        axis=0,
+    )
     grad_b = returned.T
     loss = lax.psum(loss_sum, ("sample", "feat")) / (cols_dev * blocks)
     return (loss, grad_a, grad_b)

time: 371 us -> 375 us (1.011)
  local copies, waits for them, and re-layouts: 21.2 us -> 26.2 us
    unnamed x7 -> x14, local copies, waits for them, and re-layouts: 8.63 us -> 13 us
where the time goes in v1:
time: 375 us; the launch traced here: 374 us
  waiting for transfers between devices  165 us (44%)
  blocking collectives  118 us (31%)
  matrix products  29.9 us (8%)
  local copies, waits for them, and re-layouts  26.2 us (7%)
  between operations  15.7 us (4%)
  other arithmetic  10 us (3%)
  starting transfers between devices  9.14 us (2%)
    all_gather x1, waiting for transfers between devices, body(): norm_a = lax.all_gather(local_a, 'sample', axis=0, tiled=True)  80.9 us
    psum x1, blocking collectives, body(): loss = lax.psum(loss_sum, ('sample', 'feat')) / (cols_dev * blocks)  65.5 us
    all_gather x1, waiting for transfers between devices, body(): wide_b = lax.all_gather(source_b, 'feat', axis=1, tiled=True)  53.7 us
    psum x1, blocking collectives, body(): lax.psum((jnp.sum(float_a, axis=0), jnp.sum(float_a * float_a, axis=0), j...  34.9 us
    reduce_scatter x1, waiting for transfers between devices, body(): lax.psum_scatter(lax.dot_general(factor_tile, norm_a, (((0,), (1,)), ((),...  25.1 us
    psum x1, blocking collectives, body(): lax.psum((jnp.sum(row_grad, axis=0), jnp.sum(row_grad * float_local, axis...  17.7 us
    unnamed x14, local copies, waits for them, and re-layouts  13 us
    dot_general x1, matrix products, body(): lax.dot_general(factor_tile, norm_a, (((0,), (1,)), ((), ())), preferred_...  12 us
  transfers between devices with their start and end apart: 6, of which 4 were waited for; matrix products, arithmetic and copies ran while one was open for 9% of the time, Pallas kernels for 0%

profile of v1, /device:TPU:0, one launch (start us, length us, event | category | flops | bytes accessed | tf_op | source)
XLA Modules:
  0.0 374.5 jit_solution(5703458313522905331)
XLA Ops:
  7.2 1.2 convert_reduce_fusion.2
  8.4 34.9 %all-reduce.1 = (f32[1024]{0:T(1024)S(1)}, f32[1024]{0:T(1024)S(1)}, f32[1024]{0:T(1024)S(1)}, f32[1024]{0:T(1024)S(1)}) all-reduce(f32[1024]{0:T(1024)S(1)} %get-tuple-element.23, f32[1024]{0:T(1024)S(1)} %get-tuple-element.24, f32[1024]{0:T(1024)S(1)} %get-tuple-element.8, ...), channel_id=1, replica_groups=mesh['sample'=8,'feat'=16] {'sample'}, use_global_device_ids=true, to_apply=%region_3.0 | all-reduce | flops 4096 | bytes 32768 | tf_op jit(solution)/shard_map/psum | solution.py:21
  43.4 1.7 fusion.8
  45.2 1.7 fusion.5
  46.9 53.7 %all-gather.5.cloned.1.call-done = bf16[128,16384]{1,0:T(8,128)(2,1)} async-done(((bf16[128,1024]{1,0:T(8,128)(2,1)}), bf16[128,16384]{1,0:T(8,128)(2,1)}) %all-gather.5.cloned.1.call-update) | async-done | bytes 4194320 | tf_op jit(solution)/shard_map/all_gather | solution.py:39
  100.6 5.4 %copy.11 = bf16[16,8,128,128]{3,2,1,0:T(8,128)(2,1)} copy(bf16[16,8,128,128]{3,1,2,0:T(8,128)(2,1)} %bitcast.65) | data formatting | bytes 8388608
  106.0 6.9 %copy.7 = bf16[128,16,8,128]{0,3,1,2:T(8,128)(2,1)} copy(bf16[128,16,8,128]{3,2,1,0:T(8,128)(2,1)} %bitcast.64) | data formatting | bytes 8388608 | tf_op jit(solution)/shard_map/reshape | solution.py:41
  112.9 4.6 %all-to-all-start = ((bf16[128,8,2048]{0,2,1:T(8,128)(2,1)}), bf16[128,8,2048]{0,2,1:T(8,128)(2,1)}, u32[]{:S(2)}, u32[]{:S(2)}) async-start(bf16[128,8,2048]{0,2,1:T(8,128)(2,1)} %bitcast.63), calls=%async_computation | async-start | bytes 8388608 | tf_op jit(solution)/shard_map/all_to_all | solution.py:45
  117.6 80.9 %all-gather.3.cloned.1.call-done = bf16[1024,1024]{1,0:T(8,128)(2,1)} async-done(((bf16[128,1024]{1,0:T(8,128)(2,1)}), bf16[1024,1024]{1,0:T(8,128)(2,1)}) %all-gather.3.cloned.1.call-update) | async-done | bytes 2097168 | tf_op jit(solution)/shard_map/all_gather | solution.py:37
  198.5 9.5 %select_reduce_fusion = (f32[]{:T(128)}, f32[1024,2048]{1,0:T(8,128)S(1)}) fusion(s32[2048]{0:T(1024)S(1)} %fusion.30, pred[2048]{0:T(1024)(128)(4,1)S(1)} %fusion.29, bf16[1024,1024]{1,0:T(8,128)(2,1)} %all-gather.3.cloned.1.call-done, bf16[128,8,2048]{0,2,1:T(8,128)(2,1)} %all-to-all-done), kind=kOutput, calls=%fused_computation.1 | convolution fusion | flops 4313841664 | bytes 14690308 | tf_op jit(solution)/shard_map/dot_general | solution.py:49
  208.0 3.2 copy-done.2
  211.2 8.4 %convolution_convert_fusion.1 = bf16[1024,1024]{1,0:T(8,128)(2,1)} fusion(f32[1024,2048]{1,0:T(8,128)S(1)} %get-tuple-element.22, s32[2048]{0:T(1024)S(1)} %fusion.30, pred[2048]{0:T(1024)(128)(4,1)S(1)} %fusion.29, bf16[128,8,2048]{0,2,1:T(8,128)(2,1)} %all-to-all-done), kind=kOutput, calls=%fused_computation.6 | convolution fusion | flops 4310695936 | bytes 14690304 | tf_op jit(solution)/shard_map/dot_general | solution.py:67
  219.7 12.0 %convolution_convert_fusion = bf16[2048,1024]{1,0:T(8,128)(2,1)} fusion(bf16[1024,1024]{1,0:T(8,128)(2,1)S(1)} %copy-done.1, f32[1024,2048]{1,0:T(8,128)} %copy-done.2, s32[2048]{0:T(1024)S(1)} %fusion.30, pred[2048]{0:T(1024)(128)(4,1)S(1)} %fusion.29), kind=kOutput, calls=%fused_computation.5 | convolution fusion | flops 4311744512 | bytes 14690304 | tf_op jit(solution)/shard_map/dot_general | solution.py:83
  231.8 65.5 %psum.53 = f32[]{:T(128)} all-reduce(f32[]{:T(128)} %get-tuple-element.21), channel_id=1, replica_groups=mesh['sample'=8,'feat'=16] {'sample','feat'}, use_global_device_ids=true, to_apply=%region_9.10 | all-reduce | flops 1 | bytes 8 | tf_op jit(solution)/shard_map/psum | solution.py:101
  298.0 4.8 %copy_bitcast_fusion = bf16[1024,2048]{0,1:T(8,128)(2,1)} fusion(bf16[128,8,2048]{0,2,1:T(8,128)(2,1)} %all-to-all-done), kind=kLoop, calls=%fused_computation.4 | loop fusion | bytes 8388608 | tf_op jit(solution)/shard_map/all_to_all | solution.py:45
  302.8 1.1 convert_reduce_fusion.1
  303.9 17.7 %all-reduce = (f32[1024]{0:T(1024)S(1)}, f32[1024]{0:T(1024)S(1)}) all-reduce(f32[1024]{0:T(1024)S(1)} %get-tuple-element.6, f32[1024]{0:T(1024)S(1)} %get-tuple-element.5), channel_id=1, replica_groups=mesh['sample'=8,'feat'=16] {'sample'}, use_global_device_ids=true, to_apply=%region_14.15 | all-reduce | flops 2048 | bytes 16384 | tf_op jit(solution)/shard_map/psum | solution.py:76
  321.7 25.1 %reduce-scatter.5.cloned.1.call-done = bf16[128,1024]{1,0:T(8,128)(2,1)} async-done(((bf16[2048,1024]{1,0:T(8,128)(2,1)}), bf16[128,1024]{1,0:T(8,128)(2,1)}) %reduce-scatter.5.cloned.1.call-update) | async-done | bytes 262160 | tf_op jit(solution)/shard_map/reduce_scatter | solution.py:82
  346.8 1.2 convert_reduce_fusion
  348.0 1.3 fusion.13
  354.3 4.4 %all-to-all-start.1 = ((bf16[8,128,128]{2,1,0:T(8,128)(2,1)}), bf16[8,128,128]{2,1,0:T(8,128)(2,1)S(1)}, u32[]{:S(2)}, u32[]{:S(2)}) async-start(bf16[8,128,128]{2,1,0:T(8,128)(2,1)} %fusion.15), calls=%async_computation.3 | async-start | bytes 524288 | tf_op jit(solution)/shard_map/all_to_all | solution.py:95
  358.7 1.8 fusion.3
  360.5 5.5 %all-to-all-done.1 = bf16[8,128,128]{2,1,0:T(8,128)(2,1)S(1)} async-done(((bf16[8,128,128]{2,1,0:T(8,128)(2,1)}), bf16[8,128,128]{2,1,0:T(8,128)(2,1)S(1)}, u32[]{:S(2)}, u32[]{:S(2)}) %all-to-all-start.1) | async-done | bytes 262176 | tf_op jit(solution)/shard_map/all_to_all | solution.py:95
  366.0 0.8 copy.9
  (32 shorter events, 5.4 us)
Async XLA Ops:
  7.2 93.5 %all-gather.5.cloned.1.call-start = ((), (), s32[]{:S(2)}) async-start(), calls=%async_computation.5 | async-start | bytes 4456448 | tf_op jit(solution)/shard_map/all_gather | solution.py:39
  45.1 153.4 %all-gather.3.cloned.1.call-start = ((), (), s32[]{:S(2)}) async-start(), calls=%async_computation.4 | async-start | bytes 2359296 | tf_op jit(solution)/shard_map/all_gather | solution.py:37
  112.9 85.6 %all-to-all-start = ((bf16[128,8,2048]{0,2,1:T(8,128)(2,1)}), bf16[128,8,2048]{0,2,1:T(8,128)(2,1)}, u32[]{:S(2)}, u32[]{:S(2)}) async-start(bf16[128,8,2048]{0,2,1:T(8,128)(2,1)} %bitcast.63), calls=%async_computation | async-start | bytes 8388608 | tf_op jit(solution)/shard_map/all_to_all | solution.py:45
  117.5 185.3 %reduce-scatter.3.cloned.1.call-start = ((), (), s32[]{:S(2)}) async-start(), calls=%async_computation.6 | async-start | bytes 2359296 | tf_op jit(solution)/shard_map/reduce_scatter | solution.py:72
  208.0 3.2 copy-start.2
  211.2 8.5 %copy-start.1 = (bf16[1024,1024]{1,0:T(8,128)(2,1)S(1)}, bf16[1024,1024]{1,0:T(8,128)(2,1)}, u32[]{:S(2)}) copy-start(bf16[1024,1024]{1,0:T(8,128)(2,1)} %all-gather.3.cloned.1.call-done) | copy-start | bytes 6291460
  219.7 127.1 %reduce-scatter.5.cloned.1.call-start = ((), (), s32[]{:S(2)}) async-start(), calls=%async_computation.7 | async-start | bytes 4456448 | tf_op jit(solution)/shard_map/reduce_scatter | solution.py:82
  298.0 4.8 %copy-start = (bf16[128,1024]{1,0:T(8,128)(2,1)S(1)}, bf16[128,1024]{1,0:T(8,128)(2,1)}, u32[]{:S(2)}) copy-start(bf16[128,1024]{1,0:T(8,128)(2,1)} %param.2) | copy-start | bytes 786436
  354.3 11.7 %all-to-all-start.1 = ((bf16[8,128,128]{2,1,0:T(8,128)(2,1)}), bf16[8,128,128]{2,1,0:T(8,128)(2,1)S(1)}, u32[]{:S(2)}, u32[]{:S(2)}) async-start(bf16[8,128,128]{2,1,0:T(8,128)(2,1)} %fusion.15), calls=%async_computation.3 | async-start | bytes 524288 | tf_op jit(solution)/shard_map/all_to_all | solution.py:95
Sparse Core Ops, SparseCore 0:
  45.2 55.3 all-gather.4
  102.8 95.5 all-gather.2
  219.8 43.6 reduce-scatter.2
  267.4 79.3 reduce-scatter.4
